TPU v7x, 256 devices: a whole 4x4x8 slice. The times are simulated.
256 devices in a mesh: dp: 4 (over x), expert: 8 (over z), tensor: 8 (over y, core).
Axes of the slice: x: 4, y: 4, z: 8, core: 2. Of those that a mesh axis runs over, the one named last changes fastest.
Arguments:
- tokens: bfloat16 [1024, 6144], P('expert'), may hold values from -6 to 6
- routes: int32 [1024, 2], P('expert'), may hold values from 0 to 7, all different within a row; in each aligned block of 128 rows (0 to 127, 128 to 255, ...) at most 64 rows name the same one
- logits: float32 [1024, 2], P('expert'), may hold values from -8 to 8
- grad_out: bfloat16 [1024, 6144], P('expert'), may hold values from -6 to 6
- w_gate: bfloat16 [8, 6144, 8192], P('expert', None, ('dp', 'tensor')), may hold values from -0.078125 to 0.078125
- w_up: bfloat16 [8, 6144, 8192], P('expert', None, ('dp', 'tensor')), may hold values from -0.078125 to 0.078125
- w_down: bfloat16 [8, 8192, 6144], P('expert', ('dp', 'tensor')), may hold values from -0.0625 to 0.0625
Outputs:
- output: bfloat16 [1024, 6144], P(('expert', 'tensor'))
- grad_tokens: bfloat16 [1024, 6144], P(('expert', 'tensor'))
Inputs may be any that keep to these rules, and one draw needn't show every extreme that they name: `routes`: each token names two different experts. The 128 tokens of one index of the expert axis name one expert at most 64 times, and in every draw some expert is named exactly 64 times by the tokens of some index.
All inputs are finite; a program needn't handle non-finite values.
Results may differ from a plain program's by a relative error of at most 0.015.
Values may be sent and summed in bfloat16 or wider, within the bound.
No kernel may reach another device: no remote copies, remote signals or barrier semaphores. Data moves between devices by JAX's collectives and lax.ppermute only.
A program may use at most 128 MiB of HBM per device.

v0:
```python
import jax
import jax.numpy as jnp
from jax import lax
from jax.sharding import PartitionSpec as P


def slot_targets(routes, experts, capacity):
    flat = routes.reshape(-1)
    labels = jnp.arange(experts, dtype=jnp.int32)
    onehot = (flat[:, None] == labels[None, :]).astype(jnp.int32)
    before = jnp.cumsum(onehot, axis=0) - onehot
    slot = jnp.sum(before * onehot, axis=1)
    return (flat * capacity + slot).reshape(-1, 2)


def activate(gate, up):
    sig = jax.nn.sigmoid(gate)
    return (gate * sig * up).astype(jnp.bfloat16)


def backprop(grad_hidden, gate, up):
    sig = jax.nn.sigmoid(gate)
    grad_gate = (grad_hidden * up * sig * (1.0 + gate * (1.0 - sig))).astype(jnp.bfloat16)
    grad_up = (grad_hidden * gate * sig).astype(jnp.bfloat16)
    return (grad_gate, grad_up)


def local(tokens, routes, logits, grad_out, w_gate, w_up, w_down):
    experts = lax.axis_size("expert")
    lanes = lax.axis_size("dp")
    tensor_size = lax.axis_size("tensor")
    group = lanes * tensor_size
    count, width = tokens.shape
    capacity = 4 * count // experts
    gate_w = w_gate[0]
    up_w = w_up[0]
    down_w = w_down[0]
    inner = gate_w.shape[1]
    contract_last = (((1,), (1,)), ((), ()))
    target = slot_targets(routes, experts, capacity)
    share = jax.nn.sigmoid(logits[:, 0] - logits[:, 1])
    weight_one = share[:, None]
    weight_two = (1.0 - share)[:, None]
    grad_one = (weight_one * grad_out.astype(jnp.float32)).astype(jnp.bfloat16)
    grad_two = (weight_two * grad_out.astype(jnp.float32)).astype(jnp.bfloat16)

    def project_in(flat):
        gate = jnp.dot(flat, gate_w, preferred_element_type=jnp.float32)
        up = jnp.dot(flat, up_w, preferred_element_type=jnp.float32)
        return jnp.concatenate([gate, up], axis=1)

    def project_back(flat):
        return lax.dot_general(flat, down_w, contract_last, preferred_element_type=jnp.float32)

    portion = capacity // group
    offset = lax.axis_index(("dp", "tensor")) * portion
    places = (
        jnp.arange(experts, dtype=jnp.int32)[:, None] * capacity
        + offset
        + jnp.arange(portion, dtype=jnp.int32)[None, :]
    )
    build_places = places.reshape(-1)
    first = (build_places[:, None] == target[None, :, 0]).astype(jnp.bfloat16)
    second = (build_places[:, None] == target[None, :, 1]).astype(jnp.bfloat16)
    rows_fwd = jnp.dot(first + second, tokens, preferred_element_type=jnp.float32).astype(
        jnp.bfloat16
    )
    rows_bwd = jnp.dot(first, grad_one, preferred_element_type=jnp.float32)
    rows_bwd = (rows_bwd + jnp.dot(second, grad_two, preferred_element_type=jnp.float32)).astype(
        jnp.bfloat16
    )
    rows_fwd, rows_bwd = (rows_fwd, rows_bwd)
    shape = (experts, portion, width)
    got_fwd, got_bwd = (
        lax.all_to_all(rows_fwd.reshape(shape), "expert", split_axis=0, concat_axis=0, tiled=True),
        lax.all_to_all(rows_bwd.reshape(shape), "expert", split_axis=0, concat_axis=0, tiled=True),
    )

    def move_in(arrived, project):
        piece = lax.all_gather(arrived, ("dp", "tensor"), axis=1, tiled=True)
        result = project(piece.reshape(-1, width))
        spread = result.reshape(piece.shape[0], piece.shape[1], -1)
        return spread.reshape(-1, spread.shape[2])

    share_rows = count // tensor_size
    piece_rows = share_rows // lanes
    position = jnp.arange(count, dtype=jnp.int32)
    block_index = position // piece_rows
    within = position % piece_rows
    source = (
        block_index % tensor_size * share_rows + block_index // tensor_size * piece_rows + within
    )
    slot_one = target[source, 0]
    slot_two = target[source, 1]
    first_weight = weight_one[source]
    second_weight = weight_two[source]

    def settle(term, left_weight, right_weight):
        shaped = term.astype(jnp.bfloat16).reshape(experts, capacity, width)
        back = lax.all_to_all(shaped, "expert", split_axis=0, concat_axis=0, tiled=True).reshape(
            -1, width
        )
        mixed = left_weight * back[slot_one].astype(jnp.float32) + right_weight * back[
            slot_two
        ].astype(jnp.float32)
        mixed = lax.optimization_barrier(mixed.astype(jnp.bfloat16)).astype(jnp.float32)
        summed = lax.psum_scatter(
            mixed.astype(jnp.bfloat16), ("dp", "tensor"), scatter_dimension=0, tiled=True
        )
        return summed

    projected = move_in(got_fwd, project_in)
    gate = projected[:, :inner]
    up = projected[:, inner:]
    hidden = activate(gate, up)
    out_piece = settle(
        jnp.dot(hidden, down_w, preferred_element_type=jnp.float32), first_weight, second_weight
    )
    grad_hidden = move_in(got_bwd, project_back)
    grad_gate, grad_up = backprop(grad_hidden, gate, up)
    term = lax.dot_general(grad_gate, gate_w, contract_last, preferred_element_type=jnp.float32)
    term = term + lax.dot_general(grad_up, up_w, contract_last, preferred_element_type=jnp.float32)
    grad_piece = settle(term, 1.0, 1.0)
    output, grad_tokens = (
        lax.all_gather(out_piece, "dp", axis=0, tiled=True),
        lax.all_gather(grad_piece, "dp", axis=0, tiled=True),
    )
    return (output, grad_tokens)


def solution(mesh):
    return jax.shard_map(
        local,
        mesh=mesh,
        in_specs=(
            P("expert", None),
            P("expert", None),
            P("expert", None),
            P("expert", None),
            P("expert", None, ("dp", "tensor")),
            P("expert", None, ("dp", "tensor")),
            P("expert", ("dp", "tensor"), None),
        ),
        out_specs=(P(("expert", "tensor"), None), P(("expert", "tensor"), None)),
        check_vma=False,
    )
```

profile of v0, /device:TPU:2, one launch (start us, length us, event | category | flops | bytes accessed | tf_op | source)
XLA Modules:
  0.0 627.2 jit_solution(16614282896826630612)
XLA Ops:
  10.5 1.8 convolution_convert_fusion.1
  12.4 18.7 %all_to_all.20 = bf16[8,2,6144]{2,1,0:T(2,128)(2,1)S(1)} all-to-all(bf16[8,2,6144]{2,1,0:T(2,128)(2,1)S(1)} %reshape.232), channel_id=1, replica_groups=mesh['dp'=4,'expert'=8,'tensor'=8] {'expert'}, dimensions={0} | all-to-all | bytes 393216 | tf_op jit(solution)/shard_map/all_to_all | solution.py:75
  32.7 1.9 fusion.14
  34.6 1.9 fusion
  36.6 12.2 %all_to_all.21 = bf16[8,2,6144]{2,1,0:T(2,128)(2,1)S(1)} all-to-all(bf16[8,2,6144]{2,1,0:T(2,128)(2,1)S(1)} %reshape.236), channel_id=1, replica_groups=mesh['dp'=4,'expert'=8,'tensor'=8] {'expert'}, dimensions={0} | all-to-all | bytes 393216 | tf_op jit(solution)/shard_map/all_to_all | solution.py:76
  49.6 31.8 %all-gather.5.cloned.1.call-done = bf16[8,64,6144]{2,0,1:T(8,128)(2,1)} async-done(((bf16[8,2,6144]{2,0,1:T(8,128)(2,1)}), bf16[8,64,6144]{2,0,1:T(8,128)(2,1)}) %all-gather.5.cloned.1.call-update) | async-done | bytes 6291472 | tf_op jit(solution)/shard_map/all_gather | solution.py:80
  81.4 6.2 copy.28
  87.7 2.6 fusion.11
  90.3 2.6 fusion.7
  92.9 44.5 %all-gather.7.cloned.1.call-done = bf16[8,64,6144]{2,0,1:T(8,128)(2,1)} async-done(((bf16[8,2,6144]{2,0,1:T(8,128)(2,1)}), bf16[8,64,6144]{2,0,1:T(8,128)(2,1)}) %all-gather.7.cloned.1.call-update) | async-done | bytes 6291472 | tf_op jit(solution)/shard_map/all_gather | solution.py:80
  137.4 6.4 %copy.30 = bf16[8,64,6144]{2,1,0:T(8,128)(2,1)S(1)} copy(bf16[8,64,6144]{2,0,1:T(8,128)(2,1)} %all-gather.7.cloned.1.call-done) | data formatting | bytes 12582912 | tf_op jit(solution)/shard_map/all_gather | solution.py:80
  143.8 2.3 fusion.3
  146.2 6.5 %fusion.9 = f32[512,6144]{1,0:T(8,128)} fusion(bf16[1,6144,256]{2,1,0:T(8,128)(2,1)S(1)} %copy-done, f32[512,256]{1,0:T(8,128)S(1)} %copy-done.4, f32[512,256]{1,0:T(8,128)S(1)} %fusion.3, f32[512,256]{1,0:T(8,128)S(1)} %copy-done.9), kind=kOutput, calls=%fused_computation.23 | convolution fusion | flops 1611923456 | bytes 17301504 | tf_op jit(solution)/shard_map/dot_general | solution.py:121
  152.7 9.1 %add_convert_fusion = bf16[512,6144]{1,0:T(8,128)(2,1)} fusion(f32[512,6144]{1,0:T(8,128)} %fusion.9, bf16[1,6144,256]{2,1,0:T(8,128)(2,1)S(1)} %copy-done.8, f32[512,256]{1,0:T(8,128)S(1)} %fusion.3, f32[512,256]{1,0:T(8,128)S(1)} %copy-done.4), kind=kOutput, calls=%fused_computation.8 | convolution fusion | flops 1617690624 | bytes 23068672 | tf_op jit(solution)/shard_map/dot_general | solution.py:122
  161.7 7.1 %all-to-all-start.3 = ((bf16[8,64,6144]{2,1,0:T(8,128)(2,1)}), bf16[8,64,6144]{2,1,0:T(8,128)(2,1)}, u32[]{:S(2)}, u32[]{:S(2)}) async-start(bf16[8,64,6144]{2,1,0:T(8,128)(2,1)} %bitcast.62), calls=%async_computation.3 | async-start | bytes 12582912 | tf_op jit(solution)/shard_map/all_to_all | solution.py:100
  168.9 6.3 %convolution_convert_fusion = bf16[512,6144]{1,0:T(8,128)(2,1)} fusion(bf16[1,256,6144]{2,1,0:T(8,128)(2,1)} %param.13, f32[512,256]{1,0:T(8,128)S(1)} %copy-done.10, f32[512,256]{1,0:T(8,128)S(1)} %copy-done.5), kind=kOutput, calls=%fused_computation.9 | convolution fusion | flops 1614544896 | bytes 10485760 | tf_op jit(solution)/shard_map/dot_general | solution.py:117
  175.2 135.6 %all-to-all-done.3 = bf16[8,64,6144]{2,1,0:T(8,128)(2,1)} async-done(((bf16[8,64,6144]{2,1,0:T(8,128)(2,1)}), bf16[8,64,6144]{2,1,0:T(8,128)(2,1)}, u32[]{:S(2)}, u32[]{:S(2)}) %all-to-all-start.3) | async-done | bytes 6291488 | tf_op jit(solution)/shard_map/all_to_all | solution.py:100
  310.8 4.8 all-to-all-start.1
  315.7 1.2 gather_fusion
  316.9 1.2 gather_fusion.3
  318.2 1.5 gather_fusion.1
  319.7 1.7 gather_fusion.4
  321.4 6.6 %gather_fusion.6 = bf16[128,6144]{1,0:T(8,128)(2,1)S(1)} fusion(bf16[512,6144]{1,0:T(8,128)(2,1)} %bitcast.22, s32[1024]{0:T(1024)S(1)} %pad_clamp_fusion.1), kind=kCustom, calls=%fused_computation.6 | custom fusion | bytes 3146240 | tf_op jit(solution)/shard_map/gather | solution.py:103
  328.0 6.6 %gather_fusion.7 = bf16[128,6144]{1,0:T(8,128)(2,1)S(1)} fusion(bf16[512,6144]{1,0:T(8,128)(2,1)} %bitcast.22, s32[1024]{0:T(1024)S(1)} %pad_clamp_fusion), kind=kCustom, calls=%fused_computation.7 | custom fusion | bytes 3146240 | tf_op jit(solution)/shard_map/gather | solution.py:103
  334.6 122.8 %all-to-all-done.1 = bf16[8,64,6144]{2,1,0:T(8,128)(2,1)} async-done(((bf16[8,64,6144]{2,1,0:T(8,128)(2,1)}), bf16[8,64,6144]{2,1,0:T(8,128)(2,1)}, u32[]{:S(2)}, u32[]{:S(2)}) %all-to-all-start.1) | async-done | bytes 6291488 | tf_op jit(solution)/shard_map/all_to_all | solution.py:100
  457.4 7.7 %gather_fusion.2 = bf16[128,6144]{1,0:T(8,128)(2,1)} fusion(bf16[512,6144]{1,0:T(8,128)(2,1)} %bitcast.11, s32[1024]{0:T(1024)S(1)} %pad_clamp_fusion.1), kind=kCustom, calls=%fused_computation.2 | custom fusion | bytes 3146240 | tf_op jit(solution)/shard_map/gather | solution.py:103
  465.2 7.9 %gather_fusion.5 = bf16[128,6144]{1,0:T(8,128)(2,1)} fusion(bf16[512,6144]{1,0:T(8,128)(2,1)} %bitcast.11, s32[1024]{0:T(1024)S(1)} %pad_clamp_fusion), kind=kCustom, calls=%fused_computation.5 | custom fusion | bytes 3146240 | tf_op jit(solution)/shard_map/gather | solution.py:103
  473.1 1.6 add_convert_fusion.1
  475.6 1.9 add_convert_fusion.2
  478.7 112.7 %all-reduce.7.cloned.1.call-done = (bf16[128,6144]{1,0:T(8,128)(2,1)}, bf16[128,6144]{1,0:T(8,128)(2,1)}) async-done(((bf16[128,6144]{1,0:T(8,128)(2,1)}, bf16[128,6144]{1,0:T(8,128)(2,1)}), (bf16[128,6144]{1,0:T(8,128)(2,1)}, bf16[128,6144]{1,0:T(8,128)(2,1)})) %all-reduce.7.cloned.1.call-update) | async-done | bytes 3145744
  592.4 13.6 %all-gather = bf16[4,4,6144]{2,1,0:T(4,128)(2,1)S(1)} all-gather(bf16[1,4,6144]{2,1,0:T(4,128)(2,1)S(1)} %dynamic-slice_bitcast_fusion.1), channel_id=1, replica_groups=mesh['dp'=4,'expert'=8,'tensor'=8] {'dp'}, dimensions={0}, use_global_device_ids=true | all-gather | bytes 245760 | tf_op jit(solution)/shard_map/all_gather | solution.py:125
  607.6 12.1 %all-gather.1 = bf16[4,4,6144]{2,1,0:T(4,128)(2,1)S(1)} all-gather(bf16[1,4,6144]{2,1,0:T(4,128)(2,1)S(1)} %dynamic-slice_bitcast_fusion), channel_id=1, replica_groups=mesh['dp'=4,'expert'=8,'tensor'=8] {'dp'}, dimensions={0}, use_global_device_ids=true | all-gather | bytes 245760 | tf_op jit(solution)/shard_map/all_gather | solution.py:126
  (64 shorter events, 10.8 us)
Async XLA Ops:
  7.2 80.5 %copy-start = (bf16[1,6144,256]{2,1,0:T(8,128)(2,1)S(1)}, bf16[1,6144,256]{2,1,0:T(8,128)(2,1)}, u32[]{:S(2)}) copy-start(bf16[1,6144,256]{2,1,0:T(8,128)(2,1)} %param.11) | copy-start | bytes 9437188
  7.2 74.2 %all-gather.5.cloned.1.call-start = ((), (), s32[]{:S(2)}) async-start(), calls=%async_computation.4 | async-start | bytes 6488064 | tf_op jit(solution)/shard_map/all_gather | solution.py:80
  31.9 105.5 %all-gather.7.cloned.1.call-start = ((), (), s32[]{:S(2)}) async-start(), calls=%async_computation.5 | async-start | bytes 6488064 | tf_op jit(solution)/shard_map/all_gather | solution.py:80
  87.6 2.6 copy-start.7
  137.4 6.4 %copy-start.6 = (bf16[1,256,6144]{2,1,0:T(8,128)(2,1)S(1)}, bf16[1,256,6144]{2,1,0:T(8,128)(2,1)}, u32[]{:S(2)}) copy-start(bf16[1,256,6144]{2,1,0:T(8,128)(2,1)} %param.13) | copy-start | bytes 9437188
  143.8 2.4 copy-start.4
  143.8 2.4 copy-start.9
  146.2 6.5 %copy-start.8 = (bf16[1,6144,256]{2,1,0:T(8,128)(2,1)S(1)}, bf16[1,6144,256]{2,1,0:T(8,128)(2,1)}, u32[]{:S(2)}) copy-start(bf16[1,6144,256]{2,1,0:T(8,128)(2,1)} %param.12) | copy-start | bytes 9437188
  161.7 7.2 %copy-start.5 = (f32[512,256]{1,0:T(8,128)S(1)}, f32[512,256]{1,0:T(8,128)}, u32[]{:S(2)}) copy-start(f32[512,256]{1,0:T(8,128)} %fusion.11) | copy-start | bytes 1572868
  161.7 7.2 %copy-start.10 = (f32[512,256]{1,0:T(8,128)S(1)}, f32[512,256]{1,0:T(8,128)}, u32[]{:S(2)}) copy-start(f32[512,256]{1,0:T(8,128)} %fusion.7) | copy-start | bytes 1572868
  161.7 149.0 %all-to-all-start.3 = ((bf16[8,64,6144]{2,1,0:T(8,128)(2,1)}), bf16[8,64,6144]{2,1,0:T(8,128)(2,1)}, u32[]{:S(2)}, u32[]{:S(2)}) async-start(bf16[8,64,6144]{2,1,0:T(8,128)(2,1)} %bitcast.62), calls=%async_computation.3 | async-start | bytes 12582912 | tf_op jit(solution)/shard_map/all_to_all | solution.py:100
  310.8 146.6 %all-to-all-start.1 = ((bf16[8,64,6144]{2,1,0:T(8,128)(2,1)}), bf16[8,64,6144]{2,1,0:T(8,128)(2,1)}, u32[]{:S(2)}, u32[]{:S(2)}) async-start(bf16[8,64,6144]{2,1,0:T(8,128)(2,1)} %bitcast.61), calls=%async_computation.1 | async-start | bytes 12582912 | tf_op jit(solution)/shard_map/all_to_all | solution.py:100
  315.6 275.9 %all-reduce.7.cloned.1.call-start = ((), (), s32[]{:S(2)}) async-start(), calls=%async_computation.6 | async-start | bytes 6291456
  473.1 1.6 copy-start.2
  473.1 2.4 copy-start.3
  475.6 1.9 copy-start.11
  475.6 144.9 %copy-start.1 = (bf16[1,6144,256]{2,1,0:T(8,128)(2,1)S(1)}, bf16[1,6144,256]{2,1,0:T(8,128)(2,1)}, u32[]{:S(2)}) copy-start(bf16[1,6144,256]{2,1,0:T(8,128)(2,1)} %param.11) | copy-start | bytes 9437188
Sparse Core Ops, SparseCore 0:
  32.0 49.3 all-gather.4
  84.5 52.8 all-gather.6
  477.6 113.8 all-reduce.6
where the time goes:
time: 630 us; the launch traced here: 627 us
  waiting for transfers between devices  448 us (71%)
  blocking collectives  56.7 us (9%)
  local copies, waits for them, and re-layouts  55.3 us (9%)
  matrix products  34.9 us (6%)
  between operations  14.9 us (2%)
  starting transfers between devices  12 us (2%)
    all_to_all x2, waiting for transfers between devices, settle(): lax.all_to_all(shaped, 'expert', split_axis=0, concat_axis=0, tiled=True)  258 us
    unnamed x4, waiting for transfers between devices  113 us
    all_gather x2, waiting for transfers between devices, move_in(): piece = lax.all_gather(arrived, ('dp', 'tensor'), axis=1, tiled=True)  76.3 us
    all_to_all x1, blocking collectives, local(): lax.all_to_all(rows_fwd.reshape(shape), 'expert', split_axis=0, concat_ax...  18.7 us
    gather x2, local copies, waits for them, and re-layouts, settle(): back[slot_two].astype(jnp.float32)  14.5 us
    gather x2, local copies, waits for them, and re-layouts, settle(): back[slot_one].astype(jnp.float32)  14.3 us
    all_gather x1, blocking collectives, local(): lax.all_gather(out_piece, 'dp', axis=0, tiled=True)  13.6 us
    all_gather x2, local copies, waits for them, and re-layouts, move_in(): piece = lax.all_gather(arrived, ('dp', 'tensor'), axis=1, tiled=True)  12.6 us
  transfers between devices with their start and end apart: 5, of which 5 were waited for; matrix products, arithmetic and copies ran while one was open for 7% of the time, Pallas kernels for 0%

commit v1 on v0

--- a/solution.py
+++ b/solution.py
@@ -77,7 +77,12 @@
     )
 
     def move_in(arrived, project):
-        piece = lax.all_gather(arrived, ("dp", "tensor"), axis=1, tiled=True)
+        piece = jnp.concatenate(
+            lax.all_to_all(
+                jnp.stack([arrived] * lax.axis_size(("dp", "tensor"))), ("dp", "tensor"), 0, 0
+            ),
+            axis=1,
+        )
         result = project(piece.reshape(-1, width))
         spread = result.reshape(piece.shape[0], piece.shape[1], -1)
         return spread.reshape(-1, spread.shape[2])

time: 630 us -> 742 us (1.18)
  blocking collectives: 56.7 us -> 117 us
  local copies, waits for them, and re-layouts: 55.3 us -> 95.8 us
  starting transfers between devices: 12 us -> 25.3 us
    all_gather x2 -> x0, waiting for transfers between devices: 76.3 us -> none  [move_in(): piece = lax.all_gather(arrived, ('dp', 'tensor'), axis=1, tiled=True)]
    all_to_all x1, blocking collectives: 12.2 us -> 78.1 us  [move_in(): lax.all_to_all(jnp.stack([arrived] * lax.axis_size(('dp', 'tensor'))), ('...]
    all_to_all x0 -> x2, waiting for transfers between devices: none -> 63.9 us  [the longest x1 56 us: move_in(): lax.all_to_all(jnp.stack([arrived] * lax.axis_size(('dp', 'tensor'))), ('...]
    another operation x1 -> x5, local copies, waits for them, and re-layouts: 0.01 us -> 39.2 us  [the longest x2 26.6 us: move_in(): result = project(piece.reshape(-1, width))]
    all_to_all x0 -> x2, starting transfers between devices: none -> 15.6 us  [the longest x1 8.47 us: local(): lax.all_to_all(rows_bwd.reshape(shape), 'expert', split_axis=0, concat_ax...]
    reshape x0 -> x2, local copies, waits for them, and re-layouts: none -> 13.8 us  [move_in(): jnp.concatenate(lax.all_to_all(jnp.stack([arrived] * lax.axis_size(('dp',...]
    all_gather x2 -> x0, local copies, waits for them, and re-layouts: 12.6 us -> none  [move_in(): piece = lax.all_gather(arrived, ('dp', 'tensor'), axis=1, tiled=True)]
    unnamed x4 -> x2, waiting for transfers between devices: 113 us -> 122 us
where the time goes in v1:
time: 742 us; the launch traced here: 740 us
  waiting for transfers between devices  443 us (60%)
  blocking collectives  117 us (16%)
  local copies, waits for them, and re-layouts  95.8 us (13%)
  matrix products  37.9 us (5%)
  starting transfers between devices  25.3 us (3%)
  between operations  15 us (2%)
    all_to_all x2, waiting for transfers between devices, settle(): lax.all_to_all(shaped, 'expert', split_axis=0, concat_axis=0, tiled=True)  258 us
    unnamed x2, waiting for transfers between devices  122 us
    all_to_all x1, blocking collectives, move_in(): lax.all_to_all(jnp.stack([arrived] * lax.axis_size(('dp', 'tensor'))), ('...  78.1 us
    all_to_all x1, waiting for transfers between devices, move_in(): lax.all_to_all(jnp.stack([arrived] * lax.axis_size(('dp', 'tensor'))), ('...  56 us
    another operation x2, local copies, waits for them, and re-layouts, move_in(): result = project(piece.reshape(-1, width))  26.6 us
  transfers between devices with their start and end apart: 5, of which 5 were waited for; matrix products, arithmetic and copies ran while one was open for 7% of the time, Pallas kernels for 0%

profile of v1, /device:TPU:2, one launch (start us, length us, event | category | flops | bytes accessed | tf_op | source)
XLA Modules:
  0.0 740.2 jit_solution(17582667050324831859)
XLA Ops:
  11.2 1.9 fusion.14
  13.1 1.9 fusion
  15.8 8.5 %all-to-all-start.3 = ((bf16[8,2,6144]{2,1,0:T(2,128)(2,1)}), bf16[8,2,6144]{2,1,0:T(2,128)(2,1)S(1)}, u32[]{:S(2)}, u32[]{:S(2)}) async-start(bf16[8,2,6144]{2,1,0:T(2,128)(2,1)} %reshape.240), calls=%async_computation.3 | async-start | bytes 393216 | tf_op jit(solution)/shard_map/all_to_all | solution.py:76
  26.9 7.8 %all-to-all-done.3 = bf16[8,2,6144]{2,1,0:T(2,128)(2,1)S(1)} async-done(((bf16[8,2,6144]{2,1,0:T(2,128)(2,1)}), bf16[8,2,6144]{2,1,0:T(2,128)(2,1)S(1)}, u32[]{:S(2)}, u32[]{:S(2)}) %all-to-all-start.3) | async-done | bytes 196640 | tf_op jit(solution)/shard_map/all_to_all | solution.py:76
  34.7 13.1 %all_to_all.30 = bf16[8,2,6144]{2,1,0:T(2,128)(2,1)S(1)} all-to-all(bf16[8,2,6144]{2,1,0:T(2,128)(2,1)} %reshape.236), channel_id=1, replica_groups=mesh['dp'=4,'expert'=8,'tensor'=8] {'expert'}, dimensions={0} | all-to-all | bytes 393216 | tf_op jit(solution)/shard_map/all_to_all | solution.py:75
  47.8 6.0 stack.5
  53.8 78.1 %all_to_all.31 = bf16[32,8,2,6144]{3,2,1,0:T(2,128)(2,1)} all-to-all(bf16[32,8,2,6144]{3,2,1,0:T(2,128)(2,1)S(1)} %stack.5), channel_id=1, replica_groups=mesh['dp'=4,'expert'=8,'tensor'=8] {'dp','tensor'}, dimensions={0} | all-to-all | bytes 12582912 | tf_op jit(solution)/shard_map/all_to_all | solution.py:81
  131.9 6.6 stack.4
  138.5 7.1 all-to-all-start.1
  145.7 6.8 copy.16
  152.5 13.3 %reshape_reshape.7 = bf16[512,6144]{1,0:T(8,128)(2,1)} reshape(bf16[8,32,2,6144]{3,2,1,0:T(2,128)(2,1)} %copy.16) | data formatting | bytes 12582912 | tf_op jit(solution)/shard_map/reshape;reshape | solution.py:86
  165.8 56.0 %all-to-all-done.1 = bf16[32,8,2,6144]{3,2,1,0:T(2,128)(2,1)} async-done(((bf16[32,8,2,6144]{3,2,1,0:T(2,128)(2,1)}), bf16[32,8,2,6144]{3,2,1,0:T(2,128)(2,1)}, u32[]{:S(2)}, u32[]{:S(2)}) %all-to-all-start.1) | async-done | bytes 6291488 | tf_op jit(solution)/shard_map/all_to_all | solution.py:81
  221.8 6.9 copy.15
  228.8 13.3 %reshape_reshape.6 = bf16[512,6144]{1,0:T(8,128)(2,1)} reshape(bf16[8,32,2,6144]{3,2,1,0:T(2,128)(2,1)} %copy.15) | data formatting | bytes 12582912 | tf_op jit(solution)/shard_map/reshape;reshape | solution.py:86
  242.1 4.7 fusion.11
  246.8 4.0 fusion.7
  250.9 1.8 fusion.3
  252.8 6.5 fusion.9
  259.2 9.0 %add_convert_fusion = bf16[512,6144]{1,0:T(8,128)(2,1)} fusion(f32[512,6144]{1,0:T(8,128)} %fusion.9, bf16[1,6144,256]{2,1,0:T(8,128)(2,1)S(1)} %copy-done.8, f32[512,256]{1,0:T(8,128)S(1)} %fusion.3, f32[512,256]{1,0:T(8,128)S(1)} %fusion.11), kind=kOutput, calls=%fused_computation.8 | convolution fusion | flops 1617690624 | bytes 23068672 | tf_op jit(solution)/shard_map/dot_general | solution.py:127
  268.3 4.9 all-to-all-start.5
  273.2 6.3 convolution_convert_fusion
  279.5 135.0 %all-to-all-done.5 = bf16[8,64,6144]{2,1,0:T(8,128)(2,1)} async-done(((bf16[8,64,6144]{2,1,0:T(8,128)(2,1)}), bf16[8,64,6144]{2,1,0:T(8,128)(2,1)}, u32[]{:S(2)}, u32[]{:S(2)}) %all-to-all-start.5) | async-done | bytes 6291488 | tf_op jit(solution)/shard_map/all_to_all | solution.py:105
  414.5 4.8 all-to-all-start.2
  425.2 6.6 gather_fusion.6
  431.8 6.6 gather_fusion.7
  438.4 122.8 %all-to-all-done.2 = bf16[8,64,6144]{2,1,0:T(8,128)(2,1)} async-done(((bf16[8,64,6144]{2,1,0:T(8,128)(2,1)}), bf16[8,64,6144]{2,1,0:T(8,128)(2,1)}, u32[]{:S(2)}, u32[]{:S(2)}) %all-to-all-start.2) | async-done | bytes 6291488 | tf_op jit(solution)/shard_map/all_to_all | solution.py:105
  561.2 7.8 %gather_fusion.2 = bf16[128,6144]{1,0:T(8,128)(2,1)} fusion(bf16[512,6144]{1,0:T(8,128)(2,1)} %bitcast.11, s32[1024]{0:T(1024)S(1)} %pad_clamp_fusion.1), kind=kCustom, calls=%fused_computation.2 | custom fusion | bytes 3146240 | tf_op jit(solution)/shard_map/gather | solution.py:108
  568.9 8.0 %gather_fusion.5 = bf16[128,6144]{1,0:T(8,128)(2,1)} fusion(bf16[512,6144]{1,0:T(8,128)(2,1)} %bitcast.11, s32[1024]{0:T(1024)S(1)} %pad_clamp_fusion), kind=kCustom, calls=%fused_computation.5 | custom fusion | bytes 3146240 | tf_op jit(solution)/shard_map/gather | solution.py:108
  579.4 1.9 add_convert_fusion.2
  582.5 121.8 %all-reduce.7.cloned.1.call-done = (bf16[128,6144]{1,0:T(8,128)(2,1)}, bf16[128,6144]{1,0:T(8,128)(2,1)}) async-done(((bf16[128,6144]{1,0:T(8,128)(2,1)}, bf16[128,6144]{1,0:T(8,128)(2,1)}), (bf16[128,6144]{1,0:T(8,128)(2,1)}, bf16[128,6144]{1,0:T(8,128)(2,1)})) %all-reduce.7.cloned.1.call-update) | async-done | bytes 3145744
  705.2 13.6 %all-gather = bf16[4,4,6144]{2,1,0:T(4,128)(2,1)S(1)} all-gather(bf16[1,4,6144]{2,1,0:T(4,128)(2,1)S(1)} %dynamic-slice_bitcast_fusion.1), channel_id=1, replica_groups=mesh['dp'=4,'expert'=8,'tensor'=8] {'dp'}, dimensions={0}, use_global_device_ids=true | all-gather | bytes 245760 | tf_op jit(solution)/shard_map/all_gather | solution.py:130
  720.5 12.1 %all-gather.1 = bf16[4,4,6144]{2,1,0:T(4,128)(2,1)S(1)} all-gather(bf16[1,4,6144]{2,1,0:T(4,128)(2,1)S(1)} %dynamic-slice_bitcast_fusion), channel_id=1, replica_groups=mesh['dp'=4,'expert'=8,'tensor'=8] {'dp'}, dimensions={0}, use_global_device_ids=true | all-gather | bytes 245760 | tf_op jit(solution)/shard_map/all_gather | solution.py:131
  (73 shorter events, 19.6 us)
Async XLA Ops:
  7.2 234.9 %copy-start = (bf16[1,6144,256]{2,1,0:T(8,128)(2,1)S(1)}, bf16[1,6144,256]{2,1,0:T(8,128)(2,1)}, u32[]{:S(2)}) copy-start(bf16[1,6144,256]{2,1,0:T(8,128)(2,1)} %param.11) | copy-start | bytes 9437188
  10.3 5.5 copy-start.11
  10.3 5.5 copy-start.12
  15.8 18.9 %all-to-all-start.3 = ((bf16[8,2,6144]{2,1,0:T(2,128)(2,1)}), bf16[8,2,6144]{2,1,0:T(2,128)(2,1)S(1)}, u32[]{:S(2)}, u32[]{:S(2)}) async-start(bf16[8,2,6144]{2,1,0:T(2,128)(2,1)} %reshape.240), calls=%async_computation.3 | async-start | bytes 393216 | tf_op jit(solution)/shard_map/all_to_all | solution.py:76
  138.5 83.3 %all-to-all-start.1 = ((bf16[32,8,2,6144]{3,2,1,0:T(2,128)(2,1)}), bf16[32,8,2,6144]{3,2,1,0:T(2,128)(2,1)}, u32[]{:S(2)}, u32[]{:S(2)}) async-start(bf16[32,8,2,6144]{3,2,1,0:T(2,128)(2,1)} %stack.4), calls=%async_computation.1 | async-start | bytes 12582912 | tf_op jit(solution)/shard_map/all_to_all | solution.py:81
  242.1 4.7 copy-start.2
  242.1 8.8 %slice-start = ((s8[6291456]{0:T(1024)(128)(4,1)}), s8[4194304]{0:T(1024)(128)(4,1)S(1)}, s32[]{:S(2)}) async-start(s8[6291456]{0:T(1024)(128)(4,1)} %bitcast.64), calls=%async_computation.7 | async-start | bytes 8388608
  246.8 12.4 %copy-start.5 = (f32[512,256]{1,0:T(8,128)}, f32[512,256]{1,0:T(8,128)S(1)}, u32[]{:S(2)}) copy-start(f32[512,256]{1,0:T(8,128)S(1)} %fusion.11) | copy-start | bytes 1572868
  246.8 4.0 slice-start.1
  246.8 4.0 copy-start.7
  250.9 1.8 copy-start.9
  252.7 6.5 copy-start.8
  268.3 4.9 copy-start.6
  268.3 4.9 copy-start.10
  268.3 146.3 %all-to-all-start.5 = ((bf16[8,64,6144]{2,1,0:T(8,128)(2,1)}), bf16[8,64,6144]{2,1,0:T(8,128)(2,1)}, u32[]{:S(2)}, u32[]{:S(2)}) async-start(bf16[8,64,6144]{2,1,0:T(8,128)(2,1)} %bitcast.63), calls=%async_computation.5 | async-start | bytes 12582912 | tf_op jit(solution)/shard_map/all_to_all | solution.py:105
  414.5 146.6 %all-to-all-start.2 = ((bf16[8,64,6144]{2,1,0:T(8,128)(2,1)}), bf16[8,64,6144]{2,1,0:T(8,128)(2,1)}, u32[]{:S(2)}, u32[]{:S(2)}) async-start(bf16[8,64,6144]{2,1,0:T(8,128)(2,1)} %bitcast.61), calls=%async_computation.2 | async-start | bytes 12582912 | tf_op jit(solution)/shard_map/all_to_all | solution.py:105
  419.3 285.0 %all-reduce.7.cloned.1.call-start = ((), (), s32[]{:S(2)}) async-start(), calls=%async_computation.6 | async-start | bytes 6291456
  576.9 1.6 copy-start.3
  576.9 2.4 copy-start.4
  579.3 1.9 copy-start.13
  579.4 154.0 %copy-start.1 = (bf16[1,6144,256]{2,1,0:T(8,128)(2,1)S(1)}, bf16[1,6144,256]{2,1,0:T(8,128)(2,1)}, u32[]{:S(2)}) copy-start(bf16[1,6144,256]{2,1,0:T(8,128)(2,1)} %param.11) | copy-start | bytes 9437188
Sparse Core Ops, SparseCore 0:
  581.4 122.8 all-reduce.6
